TPU v7x, 128 devices: a whole 4x4x4 slice. The times are simulated.
128 devices in a mesh: ctx: 64 (over z, x, y), wsh: 2 (over core).
Axes of the slice: x: 4, y: 4, z: 4, core: 2. Of those that a mesh axis runs over, the one named last changes fastest.
Arguments:
- block_input: bfloat16 [2, 8192, 640], P('wsh', 'ctx'), may hold values from -6 to 6
- cotangent: float32 [2, 8192, 640], P('wsh', 'ctx'), may hold values from -6 to 6
- pair_blocks: int32 [64, 2], replicated, may hold values from 0 to 127, as said below
- w_query: bfloat16 [640, 1024], P(None, 'wsh'), may hold values from -0.25 to 0.25
- w_key: bfloat16 [640, 256], P(None, 'wsh'), may hold values from -0.25 to 0.25
- w_value: bfloat16 [640, 256], P(None, 'wsh'), may hold values from -0.25 to 0.25
- w_out: bfloat16 [1024, 640], P('wsh'), may hold values from -0.1875 to 0.1875
- w_gate: bfloat16 [640, 2048], P(None, 'wsh'), may hold values from -0.25 to 0.25
- w_up: bfloat16 [640, 2048], P(None, 'wsh'), may hold values from -0.25 to 0.25
- w_down: bfloat16 [2048, 640], P('wsh'), may hold values from -0.125 to 0.125
- attn_pre_gain: bfloat16 [640], P('wsh'), may hold values from -0.3984375 to 0.59765625
- query_gain: bfloat16 [256], P('wsh'), may hold values from -0.3984375 to 0.59765625
- key_gain: bfloat16 [256], P('wsh'), may hold values from -0.3984375 to 0.59765625
- attn_post_gain: bfloat16 [640], P('wsh'), may hold values from -0.3984375 to 0.59765625
- ffw_pre_gain: bfloat16 [640], P('wsh'), may hold values from -0.3984375 to 0.59765625
- ffw_post_gain: bfloat16 [640], P('wsh'), may hold values from -0.3984375 to 0.59765625
Outputs:
- block_output: float32 [2, 8192, 640], P('wsh', 'ctx')
- input_grad: float32 [2, 8192, 640], P('wsh', 'ctx')
- w_query_grad: float32 [640, 1024], P(None, 'wsh')
- w_key_grad: float32 [640, 256], P(None, 'wsh')
- w_value_grad: float32 [640, 256], P(None, 'wsh')
- w_out_grad: float32 [1024, 640], P('wsh')
- w_gate_grad: float32 [640, 2048], P(None, 'wsh')
- w_up_grad: float32 [640, 2048], P(None, 'wsh')
- w_down_grad: float32 [2048, 640], P('wsh')
- attn_pre_gain_grad: float32 [640], P('wsh')
- query_gain_grad: float32 [256], P('wsh')
- key_gain_grad: float32 [256], P('wsh')
- attn_post_gain_grad: float32 [640], P('wsh')
- ffw_pre_gain_grad: float32 [640], P('wsh')
- ffw_post_gain_grad: float32 [640], P('wsh')
Inputs may be any that keep to these rules, and one draw needn't show every extreme that they name: `pair_blocks`: row r holds a block b and its mirror 2 * 64 - 1 - b, in the order in which index r of ctx stores them; over all rows every one of the 128 blocks appears exactly once.
All inputs are finite; a program needn't handle non-finite values.
Results may differ from a plain program's by a relative error of at most 0.018.
Values may be sent and summed in bfloat16 or wider, within the bound.
No kernel may reach another device: no remote copies, remote signals or barrier semaphores. Data moves between devices by JAX's collectives and lax.ppermute only.
A program may use at most 192 MiB of HBM per device.

v0:
```python
import jax
import jax.numpy as jnp
from jax import lax
from jax.sharding import PartitionSpec as P

HEADS = 4
HDIM = 256
epsilon = 1e-06
theta_base = 1000000.0


def rms_forward(values, gain_w):
    factor = lax.rsqrt(jnp.mean(values * values, axis=-1, keepdims=True) + epsilon)
    return (values * factor * (1.0 + gain_w), factor)


def rms_backward(values, factor, gain_w, grad_out):
    weighted = grad_out * (1.0 + gain_w)
    inner = jnp.mean(weighted * values, axis=-1, keepdims=True)
    grad_in = factor * (weighted - values * factor * factor * inner)
    grad_gain = jnp.sum((grad_out * values * factor).reshape(-1, values.shape[-1]), axis=0)
    return (grad_in, grad_gain)


def rotary_tables(positions, width):
    half_width = width // 2
    frequency = theta_base ** (-jnp.arange(half_width, dtype=jnp.float32) * 2.0 / width)
    angles = positions.astype(jnp.float32)[:, None] * frequency[None, :]
    return (jnp.cos(angles)[:, None, :], jnp.sin(angles)[:, None, :])


def rotate(values, cos_tab, sin_tab):
    half_width = values.shape[-1] // 2
    first_half = values[..., :half_width]
    second_half = values[..., half_width:]
    return jnp.concatenate(
        [
            first_half * cos_tab - second_half * sin_tab,
            second_half * cos_tab + first_half * sin_tab,
        ],
        axis=-1,
    )


def rotate_back(grads, cos_tab, sin_tab):
    half_width = grads.shape[-1] // 2
    first_half = grads[..., :half_width]
    second_half = grads[..., half_width:]
    return jnp.concatenate(
        [
            first_half * cos_tab + second_half * sin_tab,
            second_half * cos_tab - first_half * sin_tab,
        ],
        axis=-1,
    )


def block_positions(block_ids, half_rows):
    offsets = jnp.arange(half_rows, dtype=jnp.int32)
    return (block_ids[:, None] * half_rows + offsets[None, :]).reshape(-1)


def dot_f32(left, right):
    return jnp.dot(left, right, preferred_element_type=jnp.float32)


def masked_scores(query_rot, key_all, query_pos, key_pos):
    scores = jnp.einsum(
        "qhd,kd->hqk", query_rot, key_all, preferred_element_type=jnp.float32
    ) * HDIM ** (-0.5)
    return jnp.where(key_pos[None, None, :] <= query_pos[None, :, None], scores, -1e30)


def per_device(
    block_input,
    cotangent,
    pair_blocks,
    w_query,
    w_key,
    w_value,
    w_out,
    w_gate,
    w_up,
    w_down,
    attn_pre_gain,
    query_gain,
    key_gain,
    attn_post_gain,
    ffw_pre_gain,
    ffw_post_gain,
):
    row_count = block_input.shape[1]
    half_rows = row_count // 2
    my_rank = lax.axis_index("ctx")
    resid_in = block_input[0].astype(jnp.float32)
    grad_top = cotangent[0]
    my_blocks = lax.dynamic_slice_in_dim(pair_blocks, my_rank, 1, 0)[0]
    query_pos = block_positions(my_blocks, half_rows)
    key_pos = block_positions(pair_blocks.reshape(-1), half_rows)
    cos_tab, sin_tab = rotary_tables(query_pos, HDIM)
    (
        query_w,
        key_w,
        value_w,
        out_w,
        gate_w,
        up_w,
        down_w,
        gain_one,
        gain_query,
        gain_key,
        gain_two,
        gain_three,
        gain_four,
    ) = (
        lax.all_gather(w_query, "wsh", axis=1, tiled=True),
        lax.all_gather(w_key, "wsh", axis=1, tiled=True),
        lax.all_gather(w_value, "wsh", axis=1, tiled=True),
        lax.all_gather(w_out, "wsh", axis=0, tiled=True),
        lax.all_gather(w_gate, "wsh", axis=1, tiled=True),
        lax.all_gather(w_up, "wsh", axis=1, tiled=True),
        lax.all_gather(w_down, "wsh", axis=0, tiled=True),
        lax.all_gather(attn_pre_gain, "wsh", axis=0, tiled=True),
        lax.all_gather(query_gain, "wsh", axis=0, tiled=True),
        lax.all_gather(key_gain, "wsh", axis=0, tiled=True),
        lax.all_gather(attn_post_gain, "wsh", axis=0, tiled=True),
        lax.all_gather(ffw_pre_gain, "wsh", axis=0, tiled=True),
        lax.all_gather(ffw_post_gain, "wsh", axis=0, tiled=True),
    )
    gain_one = gain_one.astype(jnp.float32)
    gain_query = gain_query.astype(jnp.float32)
    gain_key = gain_key.astype(jnp.float32)
    gain_two = gain_two.astype(jnp.float32)
    normed_one, factor_one = rms_forward(resid_in, gain_one)
    attn_in = normed_one.astype(jnp.bfloat16)
    query_raw = dot_f32(attn_in, query_w).reshape(row_count, HEADS, HDIM)
    key_raw = dot_f32(attn_in, key_w)[:, None, :]
    value_bf = dot_f32(attn_in, value_w).astype(jnp.bfloat16)
    query_normed, query_factor = rms_forward(query_raw, gain_query)
    key_normed, key_factor = rms_forward(key_raw, gain_key)
    query_rot = rotate(query_normed, cos_tab, sin_tab).astype(jnp.bfloat16)
    key_rot = rotate(key_normed, cos_tab, sin_tab)[:, 0, :].astype(jnp.bfloat16)
    key_all, value_all = (
        lax.all_gather(key_rot, "ctx", axis=0, tiled=True),
        lax.all_gather(value_bf, "ctx", axis=0, tiled=True),
    )
    scores = masked_scores(query_rot, key_all, query_pos, key_pos)
    top_score = jnp.max(scores, axis=-1, keepdims=True)
    shifted = jnp.exp(scores - top_score)
    totals = jnp.sum(shifted, axis=-1, keepdims=True)
    probs = (shifted / totals).astype(jnp.bfloat16)
    log_total = top_score[..., 0] + jnp.log(totals[..., 0])
    attn_heads = jnp.einsum(
        "hqk,kd->qhd", probs, value_all, preferred_element_type=jnp.float32
    ).astype(jnp.bfloat16)
    attn_out = attn_heads.reshape(row_count, HEADS * HDIM)
    attn_proj = dot_f32(attn_out, out_w)
    normed_two, factor_two = rms_forward(attn_proj, gain_two)
    mid = resid_in + normed_two
    gain_three = gain_three.astype(jnp.float32)
    gain_four = gain_four.astype(jnp.float32)
    normed_three, factor_three = rms_forward(mid, gain_three)
    ffw_in = normed_three.astype(jnp.bfloat16)
    gate = dot_f32(ffw_in, gate_w)
    up_val = dot_f32(ffw_in, up_w)
    activated, gelu_back = jax.vjp(lambda inner: jax.nn.gelu(inner, approximate=True), gate)
    hidden = (activated * up_val).astype(jnp.bfloat16)
    ffw_proj = dot_f32(hidden, down_w)
    normed_four, factor_four = rms_forward(ffw_proj, gain_four)
    block_output = mid + normed_four
    grad_ffw, grad_gain_four = rms_backward(ffw_proj, factor_four, gain_four, grad_top)
    grad_ffw_bf = grad_ffw.astype(jnp.bfloat16)
    grad_w_down = dot_f32(hidden.T, grad_ffw_bf)
    grad_hidden = dot_f32(grad_ffw_bf, down_w.T)
    grad_gate = gelu_back(grad_hidden * up_val)[0].astype(jnp.bfloat16)
    grad_up = (grad_hidden * activated).astype(jnp.bfloat16)
    grad_w_gate = dot_f32(ffw_in.T, grad_gate)
    grad_w_up = dot_f32(ffw_in.T, grad_up)
    grad_ffw_in = dot_f32(grad_gate, gate_w.T) + dot_f32(grad_up, up_w.T)
    grad_mid_part, grad_gain_three = rms_backward(mid, factor_three, gain_three, grad_ffw_in)
    grad_mid = grad_top + grad_mid_part
    grad_proj, grad_gain_two = rms_backward(attn_proj, factor_two, gain_two, grad_mid)
    grad_proj_bf = grad_proj.astype(jnp.bfloat16)
    grad_w_out = dot_f32(attn_out.T, grad_proj_bf)
    grad_attn = dot_f32(grad_proj_bf, out_w.T).astype(jnp.bfloat16)
    grad_heads = grad_attn.reshape(row_count, HEADS, HDIM)
    delta = jnp.sum(grad_heads.astype(jnp.float32) * attn_heads.astype(jnp.float32), axis=-1).T
    scores_again = masked_scores(query_rot, key_all, query_pos, key_pos)
    probs_again = jnp.exp(scores_again - log_total[:, :, None])
    grad_probs = jnp.einsum(
        "qhd,kd->hqk", grad_heads, value_all, preferred_element_type=jnp.float32
    )
    grad_scores = (probs_again * (grad_probs - delta[:, :, None])).astype(jnp.bfloat16)
    grad_query = jnp.einsum(
        "hqk,kd->qhd", grad_scores, key_all, preferred_element_type=jnp.float32
    ) * HDIM ** (-0.5)
    grad_key_part = jnp.einsum(
        "hqk,qhd->kd", grad_scores, query_rot, preferred_element_type=jnp.float32
    ) * HDIM ** (-0.5)
    grad_value_part = jnp.einsum(
        "hqk,qhd->kd",
        probs_again.astype(jnp.bfloat16),
        grad_heads,
        preferred_element_type=jnp.float32,
    )
    kv_terms = jnp.concatenate([grad_key_part, grad_value_part], axis=1)
    kv_mine = lax.psum_scatter(kv_terms, "ctx", scatter_dimension=0, tiled=True)
    grad_key = kv_mine[:, :HDIM]
    grad_value = kv_mine[:, HDIM:]
    grad_query_raw, grad_gain_query = rms_backward(
        query_raw, query_factor, gain_query, rotate_back(grad_query, cos_tab, sin_tab)
    )
    grad_key_raw, grad_gain_key = rms_backward(
        key_raw, key_factor, gain_key, rotate_back(grad_key[:, None, :], cos_tab, sin_tab)
    )
    grad_query_bf = grad_query_raw.reshape(row_count, HEADS * HDIM).astype(jnp.bfloat16)
    grad_key_bf = grad_key_raw[:, 0, :].astype(jnp.bfloat16)
    grad_value_bf = grad_value.astype(jnp.bfloat16)
    grad_w_query = dot_f32(attn_in.T, grad_query_bf)
    grad_w_key = dot_f32(attn_in.T, grad_key_bf)
    grad_w_value = dot_f32(attn_in.T, grad_value_bf)
    grad_attn_in = (
        dot_f32(grad_query_bf, query_w.T)
        + dot_f32(grad_key_bf, key_w.T)
        + dot_f32(grad_value_bf, value_w.T)
    )
    grad_in_part, grad_gain_one = rms_backward(resid_in, factor_one, gain_one, grad_attn_in)
    input_grad = grad_mid + grad_in_part
    (
        half_query,
        half_key,
        half_value,
        half_out,
        half_gate,
        half_up,
        half_down,
        half_one,
        half_qgain,
        half_kgain,
        half_two,
        half_three,
        half_four,
    ) = (
        lax.psum_scatter(
            grad_w_query.astype(jnp.bfloat16), "wsh", scatter_dimension=1, tiled=True
        ).astype(jnp.float32),
        lax.psum_scatter(
            grad_w_key.astype(jnp.bfloat16), "wsh", scatter_dimension=1, tiled=True
        ).astype(jnp.float32),
        lax.psum_scatter(
            grad_w_value.astype(jnp.bfloat16), "wsh", scatter_dimension=1, tiled=True
        ).astype(jnp.float32),
        lax.psum_scatter(
            grad_w_out.astype(jnp.bfloat16), "wsh", scatter_dimension=0, tiled=True
        ).astype(jnp.float32),
        lax.psum_scatter(
            grad_w_gate.astype(jnp.bfloat16), "wsh", scatter_dimension=1, tiled=True
        ).astype(jnp.float32),
        lax.psum_scatter(
            grad_w_up.astype(jnp.bfloat16), "wsh", scatter_dimension=1, tiled=True
        ).astype(jnp.float32),
        lax.psum_scatter(
            grad_w_down.astype(jnp.bfloat16), "wsh", scatter_dimension=0, tiled=True
        ).astype(jnp.float32),
        lax.psum_scatter(
            grad_gain_one.astype(jnp.bfloat16), "wsh", scatter_dimension=0, tiled=True
        ).astype(jnp.float32),
        lax.psum_scatter(
            grad_gain_query.astype(jnp.bfloat16), "wsh", scatter_dimension=0, tiled=True
        ).astype(jnp.float32),
        lax.psum_scatter(
            grad_gain_key.astype(jnp.bfloat16), "wsh", scatter_dimension=0, tiled=True
        ).astype(jnp.float32),
        lax.psum_scatter(
            grad_gain_two.astype(jnp.bfloat16), "wsh", scatter_dimension=0, tiled=True
        ).astype(jnp.float32),
        lax.psum_scatter(
            grad_gain_three.astype(jnp.bfloat16), "wsh", scatter_dimension=0, tiled=True
        ).astype(jnp.float32),
        lax.psum_scatter(
            grad_gain_four.astype(jnp.bfloat16), "wsh", scatter_dimension=0, tiled=True
        ).astype(jnp.float32),
    )
    (
        sum_query,
        sum_key,
        sum_value,
        sum_out,
        sum_gate,
        sum_up,
        sum_down,
        sum_one,
        sum_qgain,
        sum_kgain,
        sum_two,
        sum_three,
        sum_four,
    ) = lax.psum(
        (
            half_query,
            half_key,
            half_value,
            half_out,
            half_gate,
            half_up,
            half_down,
            half_one,
            half_qgain,
            half_kgain,
            half_two,
            half_three,
            half_four,
        ),
        "ctx",
    )
    return (
        block_output[None],
        input_grad[None],
        sum_query,
        sum_key,
        sum_value,
        sum_out,
        sum_gate,
        sum_up,
        sum_down,
        sum_one,
        sum_qgain,
        sum_kgain,
        sum_two,
        sum_three,
        sum_four,
    )


def solution(mesh):
    return jax.shard_map(
        per_device,
        mesh=mesh,
        in_specs=(
            P("wsh", "ctx", None),
            P("wsh", "ctx", None),
            P(),
            P(None, "wsh"),
            P(None, "wsh"),
            P(None, "wsh"),
            P("wsh", None),
            P(None, "wsh"),
            P(None, "wsh"),
            P("wsh", None),
            P("wsh"),
            P("wsh"),
            P("wsh"),
            P("wsh"),
            P("wsh"),
            P("wsh"),
        ),
        out_specs=(
            P("wsh", "ctx", None),
            P("wsh", "ctx", None),
            P(None, "wsh"),
            P(None, "wsh"),
            P(None, "wsh"),
            P("wsh", None),
            P(None, "wsh"),
            P(None, "wsh"),
            P("wsh", None),
            P("wsh"),
            P("wsh"),
            P("wsh"),
            P("wsh"),
            P("wsh"),
            P("wsh"),
        ),
        check_vma=False,
    )
```

profile of v0, /device:TPU:0, one launch (start us, length us, event | category | flops | bytes accessed | tf_op | source)
XLA Modules:
  0.0 1200.0 jit_solution(14206055669539594924)
XLA Ops:
  8.0 1.3 fusion.80
  13.5 2.5 all-reduce.12
  18.0 1.9 all-gather.1
  19.9 2.2 all_gather.48
  25.9 2.3 all_gather.46
  28.9 1.8 convolution_convert_fusion.8
  33.6 1.8 all-gather.2
  35.8 4.4 broadcast_compare_fusion
  40.3 1.7 copy.61
  43.0 55.2 %all-gather.23.cloned.1.call-done = bf16[8192,1,256]{2,0,1:T(8,128)(2,1)} async-done(((bf16[128,1,256]{2,0,1:T(8,128)(2,1)}), bf16[8192,1,256]{2,0,1:T(8,128)(2,1)}) %all-gather.23.cloned.1.call-update) | async-done | bytes 4194320 | tf_op jit(solution)/shard_map/all_gather | solution.py:144
  98.1 10.4 fusion.81
  108.6 8.0 fusion.2
  116.6 51.4 %all-gather.11.cloned.1.call-done = bf16[8192,256]{1,0:T(8,128)(2,1)} async-done(((bf16[128,256]{1,0:T(8,128)(2,1)}), bf16[8192,256]{1,0:T(8,128)(2,1)}) %all-gather.11.cloned.1.call-update) | async-done | bytes 4194320 | tf_op jit(solution)/shard_map/all_gather | solution.py:145
  168.1 9.7 fusion.19
  177.8 1.3 all-gather.15.cloned.1.call-done
  179.1 1.8 multiply_reduce_fusion.11
  181.3 14.8 %all-gather.17.cloned.1.call-done = bf16[640,2048]{1,0:T(8,128)(2,1)} async-done(((bf16[640,1024]{1,0:T(8,128)(2,1)}), bf16[640,2048]{1,0:T(8,128)(2,1)}) %all-gather.17.cloned.1.call-update) | async-done | bytes 2621456 | tf_op jit(solution)/shard_map/all_gather | solution.py:120
  196.0 2.3 fusion.82
  198.4 14.7 %all-gather.19.cloned.1.call-done = bf16[640,2048]{1,0:T(8,128)(2,1)} async-done(((bf16[640,1024]{1,0:T(8,128)(2,1)}), bf16[640,2048]{1,0:T(8,128)(2,1)}) %all-gather.19.cloned.1.call-update) | async-done | bytes 2621456 | tf_op jit(solution)/shard_map/all_gather | solution.py:121
  213.0 3.5 multiply_convert_fusion.1
  216.5 13.6 %all-gather.21.cloned.1.call-done = bf16[2048,640]{1,0:T(8,128)(2,1)} async-done(((bf16[1024,640]{1,0:T(8,128)(2,1)}), bf16[2048,640]{1,0:T(8,128)(2,1)}) %all-gather.21.cloned.1.call-update) | async-done | bytes 2621456 | tf_op jit(solution)/shard_map/all_gather | solution.py:122
  230.1 2.6 multiply_reduce_fusion.9
  232.7 1.7 fusion.49
  234.4 1.9 multiply_convert_fusion.4
  236.3 1.4 multiply_convert_fusion
  241.6 11.6 convolution_bitcast_fusion
  253.2 8.8 fusion.1
  262.0 3.8 fusion.4
  266.3 2.3 copy-done.1
  268.6 6.3 pad_maximum_fusion
  274.9 8.0 fusion.16
  284.1 1.7 convolution_convert_fusion.4
  285.9 1.5 convolution_convert_fusion.3
  287.6 2.4 convolution_convert_fusion.2
  290.2 2.4 convolution_convert_fusion.1
  292.7 2.4 convolution_convert_fusion
  296.5 367.4 %reduce-scatter.13.cloned.1.call-done = f32[128,512]{1,0:T(8,128)} async-done(((f32[8192,512]{1,0:T(8,128)}), f32[128,512]{1,0:T(8,128)}) %reduce-scatter.13.cloned.1.call-update) | async-done | bytes 262160 | tf_op jit(solution)/shard_map/reduce_scatter | solution.py:207
  667.4 6.5 reduce-scatter.15.cloned.1.call-done
  674.0 15.7 %reduce-scatter.17.cloned.1.call-done = bf16[512,640]{1,0:T(8,128)(2,1)} async-done(((bf16[1024,640]{1,0:T(8,128)(2,1)}), bf16[512,640]{1,0:T(8,128)(2,1)}) %reduce-scatter.17.cloned.1.call-update) | async-done | bytes 655376 | tf_op jit(solution)/shard_map/reduce_scatter | solution.py:253
  689.7 17.2 %reduce-scatter.19.cloned.1.call-done = bf16[640,1024]{1,0:T(8,128)(2,1)} async-done(((bf16[640,2048]{1,0:T(8,128)(2,1)}), bf16[640,1024]{1,0:T(8,128)(2,1)}) %reduce-scatter.19.cloned.1.call-update) | async-done | bytes 1310736 | tf_op jit(solution)/shard_map/reduce_scatter | solution.py:256
  707.0 17.2 %reduce-scatter.21.cloned.1.call-done = bf16[640,1024]{1,0:T(8,128)(2,1)} async-done(((bf16[640,2048]{1,0:T(8,128)(2,1)}), bf16[640,1024]{1,0:T(8,128)(2,1)}) %reduce-scatter.21.cloned.1.call-update) | async-done | bytes 1310736 | tf_op jit(solution)/shard_map/reduce_scatter | solution.py:259
  724.2 17.2 %reduce-scatter.23.cloned.1.call-done = bf16[1024,640]{1,0:T(8,128)(2,1)} async-done(((bf16[2048,640]{1,0:T(8,128)(2,1)}), bf16[1024,640]{1,0:T(8,128)(2,1)}) %reduce-scatter.23.cloned.1.call-update) | async-done | bytes 1310736 | tf_op jit(solution)/shard_map/reduce_scatter | solution.py:262
  743.0 2.1 fusion.45
  745.1 2.6 all-reduce.11
  747.9 1.8 fusion.41
  749.8 5.8 reduce-scatter.25.cloned.1.call-done
  756.6 13.5 %reduce-scatter.27.cloned.1.call-done = bf16[128,640]{1,0:T(8,128)(2,1)} async-done(((bf16[256,640]{1,0:T(8,128)(2,1)}), bf16[128,640]{1,0:T(8,128)(2,1)}) %reduce-scatter.27.cloned.1.call-update) | async-done | bytes 163856
  771.2 422.1 %all-reduce.14 = (f32[640,512]{1,0:T(8,128)}, f32[640,128]{1,0:T(8,128)}, f32[640,128]{1,0:T(8,128)}, f32[512,640]{1,0:T(8,128)}, f32[640,1024]{1,0:T(8,128)}, /...) all-reduce(bf16[640,512]{1,0:T(8,128)(2,1)} %reduce-scatter.15.clon, ...), channel_id=1, replica_groups=mesh['ctx'=64,'wsh'=2] {'ctx'}, use_global_device_ids=true, to_apply=%region_17.18 | all-reduce | flops 2786816 | bytes 16723968 | tf_op jit(solution)/shard_map/psum | solution.py:298
  (202 shorter events, 28.7 us)
Async XLA Ops:
  7.2 26.4 %copy-start.46 = (s32[64,2]{0,1:T(2,128)S(1)}, s32[64,2]{0,1:T(2,128)}, u32[]{:S(2)}) copy-start(s32[64,2]{0,1:T(2,128)} %param.18) | copy-start | bytes 1540
  7.2 26.5 %copy-start.48 = (bf16[128]{0:T(256)(128)(2,1)S(1)}, bf16[128]{0:T(256)(128)(2,1)}, u32[]{:S(2)}) copy-start(bf16[128]{0:T(256)(128)(2,1)} %param.27) | copy-start | bytes 772
  7.2 33.1 %all-gather.13.cloned.1.call-start = ((), (), s32[]{:S(2)}) async-start(), calls=%async_computation.9 | async-start | bytes 1966080 | tf_op jit(solution)/shard_map/all_gather | solution.py:116
  7.9 90.2 %all-gather.23.cloned.1.call-start = ((), (), s32[]{:S(2)}) async-start(), calls=%async_computation.20 | async-start | bytes 4259840 | tf_op jit(solution)/shard_map/all_gather | solution.py:144
  8.0 32.2 %copy-start.40 = (f32[128]{0:T(128)}, f32[128]{0:T(128)S(1)}, u32[]{:S(2)}) copy-start(f32[128]{0:T(128)S(1)} %multiply_power_fusion) | copy-start | bytes 1540
  18.0 22.2 %copy-start.44 = (f32[128]{0:T(128)}, f32[128]{0:T(128)S(1)}, u32[]{:S(2)}) copy-start(f32[128]{0:T(128)S(1)} %convert_element_type.193) | copy-start | bytes 1540
  24.2 17.9 %copy-start.42 = (f32[128]{0:T(128)}, f32[128]{0:T(128)S(1)}, u32[]{:S(2)}) copy-start(f32[128]{0:T(128)S(1)} %add_rsqrt_fusion.4) | copy-start | bytes 1540
  25.9 142.2 %all-gather.11.cloned.1.call-start = ((), (), s32[]{:S(2)}) async-start(), calls=%async_computation.8 | async-start | bytes 4259840 | tf_op jit(solution)/shard_map/all_gather | solution.py:145
  30.7 11.3 copy-start.4
  30.7 148.4 %all-gather.15.cloned.1.call-start = ((), (), s32[]{:S(2)}) async-start(), calls=%async_computation.10 | async-start | bytes 1966080 | tf_op jit(solution)/shard_map/all_gather | solution.py:119
  31.3 164.7 %all-gather.17.cloned.1.call-start = ((), (), s32[]{:S(2)}) async-start(), calls=%async_computation.11 | async-start | bytes 3932160 | tf_op jit(solution)/shard_map/all_gather | solution.py:120
  31.9 181.1 %all-gather.19.cloned.1.call-start = ((), (), s32[]{:S(2)}) async-start(), calls=%async_computation.12 | async-start | bytes 3932160 | tf_op jit(solution)/shard_map/all_gather | solution.py:121
  32.5 197.6 %all-gather.21.cloned.1.call-start = ((), (), s32[]{:S(2)}) async-start(), calls=%async_computation.13 | async-start | bytes 3932160 | tf_op jit(solution)/shard_map/all_gather | solution.py:122
  33.2 630.6 %reduce-scatter.13.cloned.1.call-start = ((), (), s32[]{:S(2)}) async-start(), calls=%async_computation.14 | async-start | bytes 17039360 | tf_op jit(solution)/shard_map/reduce_scatter | solution.py:207
  33.6 75.0 %copy-start.32 = (f32[128,128]{1,0:T(8,128)}, f32[128,128]{1,0:T(8,128)S(1)}, u32[]{:S(2)}) copy-start(f32[128,128]{1,0:T(8,128)S(1)} %get-tuple-element.65) | copy-start | bytes 196612
  33.6 75.0 %copy-start.34 = (f32[128,128]{1,0:T(8,128)}, f32[128,128]{1,0:T(8,128)S(1)}, u32[]{:S(2)}) copy-start(f32[128,128]{1,0:T(8,128)S(1)} %get-tuple-element.66) | copy-start | bytes 196612
  42.9 65.7 %copy-start.37 = (bf16[128,4,128]{2,0,1:T(8,128)(2,1)}, bf16[128,4,128]{2,0,1:T(8,128)(2,1)S(1)}, u32[]{:S(2)}) copy-start(bf16[128,4,128]{2,0,1:T(8,128)(2,1)S(1)} %get-tuple-element.57) | copy-start | bytes 393220
  42.9 65.7 %copy-start.38 = (bf16[128,4,128]{2,0,1:T(8,128)(2,1)}, bf16[128,4,128]{2,0,1:T(8,128)(2,1)S(1)}, u32[]{:S(2)}) copy-start(bf16[128,4,128]{2,0,1:T(8,128)(2,1)S(1)} %get-tuple-element.58) | copy-start | bytes 393220
  181.3 35.2 %copy-start.7 = (bf16[128,640]{1,0:T(8,128)(2,1)}, bf16[128,640]{1,0:T(8,128)(2,1)S(1)}, u32[]{:S(2)}) copy-start(bf16[128,640]{1,0:T(8,128)(2,1)S(1)} %multiply_convert_fusion.5) | copy-start | bytes 491524
  230.1 6.1 copy-start.12
  230.1 6.1 copy-start.29
  240.6 12.6 %copy-start.10 = (f32[128,640]{1,0:T(8,128)}, f32[128,640]{1,0:T(8,128)S(1)}, u32[]{:S(2)}) copy-start(f32[128,640]{1,0:T(8,128)S(1)} %get-tuple-element.50) | copy-start | bytes 983044
  240.8 12.4 %copy-start.20 = (bf16[128,640]{1,0:T(8,128)(2,1)}, bf16[128,640]{1,0:T(8,128)(2,1)S(1)}, u32[]{:S(2)}) copy-start(bf16[128,640]{1,0:T(8,128)(2,1)S(1)} %multiply_convert_fusion.3) | copy-start | bytes 491524
  262.0 4.3 copy-start
  262.0 6.5 copy-start.1
  274.8 8.1 copy-start.33
  274.8 8.1 copy-start.35
  274.9 399.1 %reduce-scatter.15.cloned.1.call-start = ((), (), s32[]{:S(2)}) async-start(), calls=%async_computation.15 | async-start | bytes 1966080 | tf_op jit(solution)/shard_map/reduce_scatter | solution.py:244
  283.7 3.8 copy-start.19
  285.8 4.4 copy-start.17
  285.9 403.9 %reduce-scatter.17.cloned.1.call-start = ((), (), s32[]{:S(2)}) async-start(), calls=%async_computation.16 | async-start | bytes 1966080 | tf_op jit(solution)/shard_map/reduce_scatter | solution.py:253
  287.5 419.5 %reduce-scatter.19.cloned.1.call-start = ((), (), s32[]{:S(2)}) async-start(), calls=%async_computation.17 | async-start | bytes 3932160 | tf_op jit(solution)/shard_map/reduce_scatter | solution.py:256
  290.0 434.2 %reduce-scatter.21.cloned.1.call-start = ((), (), s32[]{:S(2)}) async-start(), calls=%async_computation.18 | async-start | bytes 3932160 | tf_op jit(solution)/shard_map/reduce_scatter | solution.py:259
  292.6 372.3 %copy-start.41 = (f32[128]{0:T(128)S(1)}, f32[128]{0:T(128)}, u32[]{:S(2)}) copy-start(f32[128]{0:T(128)} %copy-done.40) | copy-start | bytes 1540
  292.6 372.3 %copy-start.45 = (f32[128]{0:T(128)S(1)}, f32[128]{0:T(128)}, u32[]{:S(2)}) copy-start(f32[128]{0:T(128)} %copy-done.44) | copy-start | bytes 1540
  292.6 372.7 %copy-start.28 = (f32[128,256]{1,0:T(8,128)S(1)}, f32[128,256]{1,0:T(8,128)}, u32[]{:S(2)}) copy-start(f32[128,256]{1,0:T(8,128)} %copy-done.27) | copy-start | bytes 393220
  292.6 372.7 %copy-start.43 = (f32[128]{0:T(128)S(1)}, f32[128]{0:T(128)}, u32[]{:S(2)}) copy-start(f32[128]{0:T(128)} %copy-done.42) | copy-start | bytes 1540
  292.6 374.3 %copy-start.5 = (bf16[640,1024]{1,0:T(8,128)(2,1)S(1)}, bf16[640,1024]{1,0:T(8,128)(2,1)}, u32[]{:S(2)}) copy-start(bf16[640,1024]{1,0:T(8,128)(2,1)} %all-gather.13.cloned.1.call-done) | copy-start | bytes 3932164
  292.6 448.8 %reduce-scatter.23.cloned.1.call-start = ((), (), s32[]{:S(2)}) async-start(), calls=%async_computation.19 | async-start | bytes 3932160 | tf_op jit(solution)/shard_map/reduce_scatter | solution.py:262
  295.1 447.6 %copy-start.23 = (bf16[640,256]{1,0:T(8,128)(2,1)S(1)}, bf16[640,256]{1,0:T(8,128)(2,1)}, u32[]{:S(2)}) copy-start(bf16[640,256]{1,0:T(8,128)(2,1)} %copy-done.22) | copy-start | bytes 983044
  295.1 460.4 %reduce-scatter.25.cloned.1.call-start = ((), (), s32[]{:S(2)}) async-start(), calls=%async_computation.21 | async-start | bytes 491520
  663.9 77.5 %copy-start.36 = (f32[128,512]{1,0:T(8,128)S(1)}, f32[128,512]{1,0:T(8,128)}, u32[]{:S(2)}) copy-start(f32[128,512]{1,0:T(8,128)} %reduce-scatter.13.cloned.1.call-done) | copy-start | bytes 786436
  664.9 80.2 %copy-start.39 = (bf16[640]{0:T(1024)(128)(2,1)S(1)}, bf16[640]{0:T(1024)(128)(2,1)}, u32[]{:S(2)}) copy-start(bf16[640]{0:T(1024)(128)(2,1)} %get-tuple-element.17) | copy-start | bytes 3844
  664.9 80.2 %copy-start.47 = (bf16[256]{0:T(256)(128)(2,1)S(1)}, bf16[256]{0:T(256)(128)(2,1)}, u32[]{:S(2)}) copy-start(bf16[256]{0:T(256)(128)(2,1)} %get-tuple-element.15) | copy-start | bytes 1540
  664.9 83.0 %copy-start.11 = (f32[128,640]{1,0:T(8,128)S(1)}, f32[128,640]{1,0:T(8,128)}, u32[]{:S(2)}) copy-start(f32[128,640]{1,0:T(8,128)} %copy-done.10) | copy-start | bytes 983044
  666.8 103.2 %reduce-scatter.27.cloned.1.call-start = ((), (), s32[]{:S(2)}) async-start(), calls=%async_computation.22 | async-start | bytes 491520
  707.0 64.2 %copy-start.24 = (bf16[640,1024]{1,0:T(8,128)(2,1)S(1)}, bf16[640,1024]{1,0:T(8,128)(2,1)}, u32[]{:S(2)}) copy-start(bf16[640,1024]{1,0:T(8,128)(2,1)} %reduce-scatter.19.cloned.1.call-done) | copy-start | bytes 3932164
  742.9 28.2 %copy-start.25 = (bf16[640,1024]{1,0:T(8,128)(2,1)S(1)}, bf16[640,1024]{1,0:T(8,128)(2,1)}, u32[]{:S(2)}) copy-start(bf16[640,1024]{1,0:T(8,128)(2,1)} %reduce-scatter.21.cloned.1.call-done) | copy-start | bytes 3932164
  (16 other events, 37.4 us)
Sparse Core Ops, SparseCore 0:
  9.7 14.5 all-gather.12
  27.7 70.3 all-gather.22
  101.6 66.4 all-gather.10
  169.6 9.5 all-gather.14
  180.6 15.3 all-gather.16
  197.6 15.4 all-gather.18
  214.7 15.3 all-gather.20
  275.0 388.8 reduce-scatter.12
  666.8 7.1 reduce-scatter.14
  676.9 12.8 reduce-scatter.16
  692.7 14.2 reduce-scatter.18
  709.9 14.2 reduce-scatter.20
  727.1 14.2 reduce-scatter.22
  743.7 11.7 reduce-scatter.24
  758.3 11.7 reduce-scatter.26
where the time goes:
time: 1210 us; the launch traced here: 1200 us
  waiting for transfers between devices  615 us (51%)
  blocking collectives  435 us (36%)
  matrix products  84 us (7%)
  other arithmetic  30.5 us (3%)
  local copies, waits for them, and re-layouts  17.7 us (1%)
  between operations  17 us (1%)
    psum x1, blocking collectives, per_device(): lax.psum((half_query, half_key, half_value, half_out, half_gate, half_up,...  422 us
    reduce_scatter x1, waiting for transfers between devices, per_device(): kv_mine = lax.psum_scatter(kv_terms, 'ctx', scatter_dimension=0, tiled=True)  367 us
    all_gather x1, waiting for transfers between devices, per_device(): lax.all_gather(key_rot, 'ctx', axis=0, tiled=True)  55.2 us
    all_gather x1, waiting for transfers between devices, per_device(): lax.all_gather(value_bf, 'ctx', axis=0, tiled=True)  51.4 us
    dot_general x21, matrix products, dot_f32(): return jnp.dot(left, right, preferred_element_type=jnp.float32)  31.7 us
  transfers between devices with their start and end apart: 15, of which 14 were waited for; matrix products, arithmetic and copies ran while one was open for 7% of the time, Pallas kernels for 0%

commit v1 on v0

--- a/solution.py
+++ b/solution.py
@@ -141,7 +141,9 @@
     query_rot = rotate(query_normed, cos_tab, sin_tab).astype(jnp.bfloat16)
     key_rot = rotate(key_normed, cos_tab, sin_tab)[:, 0, :].astype(jnp.bfloat16)
     key_all, value_all = (
-        lax.all_gather(key_rot, "ctx", axis=0, tiled=True),
+        jnp.concatenate(
+            lax.all_to_all(jnp.stack(lax.axis_size("ctx") * [key_rot], axis=0), "ctx", 0, 0), axis=0
+        ),
         lax.all_gather(value_bf, "ctx", axis=0, tiled=True),
     )
     scores = masked_scores(query_rot, key_all, query_pos, key_pos)

time: 1210 us -> 1180 us (0.975)
  waiting for transfers between devices: 615 us -> 572 us
    all_gather x1 -> x0, waiting for transfers between devices: 55.2 us -> none  [per_device(): lax.all_gather(key_rot, 'ctx', axis=0, tiled=True)]
    all_to_all x0 -> x1, waiting for transfers between devices: none -> 44.9 us  [per_device(): lax.all_to_all(jnp.stack(lax.axis_size('ctx') * [key_rot], axis=0), 'ctx'...]
    all_gather x1, waiting for transfers between devices: 51.4 us -> 20.1 us  [per_device(): lax.all_gather(value_bf, 'ctx', axis=0, tiled=True)]
where the time goes in v1:
time: 1180 us; the launch traced here: 1170 us
  waiting for transfers between devices  572 us (48%)
  blocking collectives  435 us (37%)
  matrix products  83.1 us (7%)
  other arithmetic  29.3 us (2%)
  local copies, waits for them, and re-layouts  19.5 us (2%)
  between operations  17 us (1%)
  starting transfers between devices  12.7 us (1%)
    psum x1, blocking collectives, per_device(): lax.psum((half_query, half_key, half_value, half_out, half_gate, half_up,...  422 us
    reduce_scatter x1, waiting for transfers between devices, per_device(): kv_mine = lax.psum_scatter(kv_terms, 'ctx', scatter_dimension=0, tiled=True)  368 us
    all_to_all x1, waiting for transfers between devices, per_device(): lax.all_to_all(jnp.stack(lax.axis_size('ctx') * [key_rot], axis=0), 'ctx'...  44.9 us
    dot_general x21, matrix products, dot_f32(): return jnp.dot(left, right, preferred_element_type=jnp.float32)  30.8 us
  transfers between devices with their start and end apart: 15, of which 14 were waited for; matrix products, arithmetic and copies ran while one was open for 7% of the time, Pallas kernels for 0%

profile of v1, /device:TPU:0, one launch (start us, length us, event | category | flops | bytes accessed | tf_op | source)
XLA Modules:
  0.0 1168.7 jit_solution(2612246335440572044)
XLA Ops:
  13.4 2.5 all-reduce.12
  15.9 2.2 all_gather.43
  19.3 1.8 convolution_convert_fusion.8
  23.4 1.8 all-gather
  25.2 2.0 all_gather.45
  29.4 2.5 stack.2
  31.9 11.9 %all-to-all-start = ((bf16[64,128,256]{2,1,0:T(8,128)(2,1)}), bf16[64,128,256]{2,1,0:T(8,128)(2,1)}, u32[]{:S(2)}, u32[]{:S(2)}) async-start(bf16[64,128,256]{2,1,0:T(8,128)(2,1)} %stack.2), calls=%async_computation | async-start | bytes 8388608 | tf_op jit(solution)/shard_map/all_to_all | solution.py:145
  44.9 1.8 all-gather.1
  47.0 4.5 broadcast_compare_fusion
  51.5 1.7 copy.61
  54.1 44.9 %all-to-all-done = bf16[64,128,256]{2,1,0:T(8,128)(2,1)} async-done(((bf16[64,128,256]{2,1,0:T(8,128)(2,1)}), bf16[64,128,256]{2,1,0:T(8,128)(2,1)}, u32[]{:S(2)}, u32[]{:S(2)}) %all-to-all-start) | async-done | bytes 4194336 | tf_op jit(solution)/shard_map/all_to_all | solution.py:145
  99.0 10.5 fusion.73
  109.5 8.0 fusion.2
  117.5 20.1 %all-gather.9.cloned.1.call-done = bf16[8192,256]{1,0:T(8,128)(2,1)} async-done(((bf16[128,256]{1,0:T(8,128)(2,1)}), bf16[8192,256]{1,0:T(8,128)(2,1)}) %all-gather.9.cloned.1.call-update) | async-done | bytes 4194320 | tf_op jit(solution)/shard_map/all_gather | solution.py:147
  137.6 9.7 fusion.11
  147.3 1.5 all-gather.13.cloned.1.call-done
  148.8 1.8 multiply_reduce_fusion.11
  150.9 14.8 %all-gather.15.cloned.1.call-done = bf16[640,2048]{1,0:T(8,128)(2,1)} async-done(((bf16[640,1024]{1,0:T(8,128)(2,1)}), bf16[640,2048]{1,0:T(8,128)(2,1)}) %all-gather.15.cloned.1.call-update) | async-done | bytes 2621456 | tf_op jit(solution)/shard_map/all_gather | solution.py:120
  165.7 2.3 fusion.74
  168.0 14.7 %all-gather.17.cloned.1.call-done = bf16[640,2048]{1,0:T(8,128)(2,1)} async-done(((bf16[640,1024]{1,0:T(8,128)(2,1)}), bf16[640,2048]{1,0:T(8,128)(2,1)}) %all-gather.17.cloned.1.call-update) | async-done | bytes 2621456 | tf_op jit(solution)/shard_map/all_gather | solution.py:121
  182.7 3.5 multiply_convert_fusion.1
  186.2 13.4 %all-gather.19.cloned.1.call-done = bf16[2048,640]{1,0:T(8,128)(2,1)} async-done(((bf16[1024,640]{1,0:T(8,128)(2,1)}), bf16[2048,640]{1,0:T(8,128)(2,1)}) %all-gather.19.cloned.1.call-update) | async-done | bytes 2621456 | tf_op jit(solution)/shard_map/all_gather | solution.py:122
  199.6 2.6 multiply_reduce_fusion.9
  202.2 1.7 fusion.41
  203.9 1.9 multiply_convert_fusion.4
  211.1 11.6 convolution_bitcast_fusion
  222.7 8.8 fusion.1
  231.5 3.8 fusion.4
  235.8 2.3 copy-done.1
  238.1 6.3 pad_maximum_fusion
  244.4 8.0 fusion.10
  253.7 1.7 convolution_convert_fusion.4
  255.4 1.5 convolution_convert_fusion.3
  257.1 2.4 convolution_convert_fusion.2
  259.7 2.4 convolution_convert_fusion.1
  262.2 2.4 convolution_convert_fusion
  266.0 367.7 %reduce-scatter.13.cloned.1.call-done = f32[128,512]{1,0:T(8,128)} async-done(((f32[8192,512]{1,0:T(8,128)}), f32[128,512]{1,0:T(8,128)}) %reduce-scatter.13.cloned.1.call-update) | async-done | bytes 262160 | tf_op jit(solution)/shard_map/reduce_scatter | solution.py:209
  637.2 5.5 reduce-scatter.15.cloned.1.call-done
  642.7 15.9 %reduce-scatter.17.cloned.1.call-done = bf16[512,640]{1,0:T(8,128)(2,1)} async-done(((bf16[1024,640]{1,0:T(8,128)(2,1)}), bf16[512,640]{1,0:T(8,128)(2,1)}) %reduce-scatter.17.cloned.1.call-update) | async-done | bytes 655376 | tf_op jit(solution)/shard_map/reduce_scatter | solution.py:255
  658.6 17.1 %reduce-scatter.19.cloned.1.call-done = bf16[640,1024]{1,0:T(8,128)(2,1)} async-done(((bf16[640,2048]{1,0:T(8,128)(2,1)}), bf16[640,1024]{1,0:T(8,128)(2,1)}) %reduce-scatter.19.cloned.1.call-update) | async-done | bytes 1310736 | tf_op jit(solution)/shard_map/reduce_scatter | solution.py:258
  675.7 17.4 %reduce-scatter.21.cloned.1.call-done = bf16[640,1024]{1,0:T(8,128)(2,1)} async-done(((bf16[640,2048]{1,0:T(8,128)(2,1)}), bf16[640,1024]{1,0:T(8,128)(2,1)}) %reduce-scatter.21.cloned.1.call-update) | async-done | bytes 1310736 | tf_op jit(solution)/shard_map/reduce_scatter | solution.py:261
  693.1 17.1 %reduce-scatter.23.cloned.1.call-done = bf16[1024,640]{1,0:T(8,128)(2,1)} async-done(((bf16[2048,640]{1,0:T(8,128)(2,1)}), bf16[1024,640]{1,0:T(8,128)(2,1)}) %reduce-scatter.23.cloned.1.call-update) | async-done | bytes 1310736 | tf_op jit(solution)/shard_map/reduce_scatter | solution.py:264
  711.7 2.1 fusion.37
  713.8 2.6 all-reduce.11
  716.6 1.8 fusion.33
  718.5 5.9 reduce-scatter.25.cloned.1.call-done
  725.5 13.5 %reduce-scatter.27.cloned.1.call-done = bf16[128,640]{1,0:T(8,128)(2,1)} async-done(((bf16[256,640]{1,0:T(8,128)(2,1)}), bf16[128,640]{1,0:T(8,128)(2,1)}) %reduce-scatter.27.cloned.1.call-update) | async-done | bytes 163856
  740.1 421.9 %all-reduce.14 = (f32[640,512]{1,0:T(8,128)}, f32[640,128]{1,0:T(8,128)}, f32[640,128]{1,0:T(8,128)}, f32[512,640]{1,0:T(8,128)}, f32[640,1024]{1,0:T(8,128)}, /...) all-reduce(bf16[640,512]{1,0:T(8,128)(2,1)} %reduce-scatter.15.clon, ...), channel_id=1, replica_groups=mesh['ctx'=64,'wsh'=2] {'ctx'}, use_global_device_ids=true, to_apply=%region_17.18 | all-reduce | flops 2786816 | bytes 16723968 | tf_op jit(solution)/shard_map/psum | solution.py:300
  (206 shorter events, 28.4 us)
Async XLA Ops:
  7.2 20.8 %copy-start.4 = (bf16[1,128,640]{2,1,0:T(8,128)(2,1)S(1)}, bf16[1,128,640]{2,1,0:T(8,128)(2,1)}, u32[]{:S(2)}) copy-start(bf16[1,128,640]{2,1,0:T(8,128)(2,1)} %param.16) | copy-start | bytes 491524
  7.2 15.9 %copy-start.47 = (s32[64,2]{0,1:T(2,128)S(1)}, s32[64,2]{0,1:T(2,128)}, u32[]{:S(2)}) copy-start(s32[64,2]{0,1:T(2,128)} %param.18) | copy-start | bytes 1540
  7.2 16.2 %copy-start.49 = (bf16[128]{0:T(256)(128)(2,1)S(1)}, bf16[128]{0:T(256)(128)(2,1)}, u32[]{:S(2)}) copy-start(bf16[128]{0:T(256)(128)(2,1)} %param.28) | copy-start | bytes 772
  7.2 18.0 %copy-start.39 = (bf16[640,128]{1,0:T(8,128)(2,1)S(1)}, bf16[640,128]{1,0:T(8,128)(2,1)}, u32[]{:S(2)}) copy-start(bf16[640,128]{1,0:T(8,128)(2,1)} %param.20) | copy-start | bytes 491524
  7.2 44.2 %all-gather.11.cloned.1.call-start = ((), (), s32[]{:S(2)}) async-start(), calls=%async_computation.10 | async-start | bytes 1966080 | tf_op jit(solution)/shard_map/all_gather | solution.py:116
  8.0 129.6 %all-gather.9.cloned.1.call-start = ((), (), s32[]{:S(2)}) async-start(), calls=%async_computation.9 | async-start | bytes 4259840 | tf_op jit(solution)/shard_map/all_gather | solution.py:147
  21.2 127.6 %all-gather.13.cloned.1.call-start = ((), (), s32[]{:S(2)}) async-start(), calls=%async_computation.11 | async-start | bytes 1966080 | tf_op jit(solution)/shard_map/all_gather | solution.py:119
  21.9 143.8 %all-gather.15.cloned.1.call-start = ((), (), s32[]{:S(2)}) async-start(), calls=%async_computation.12 | async-start | bytes 3932160 | tf_op jit(solution)/shard_map/all_gather | solution.py:120
  22.5 160.2 %all-gather.17.cloned.1.call-start = ((), (), s32[]{:S(2)}) async-start(), calls=%async_computation.13 | async-start | bytes 3932160 | tf_op jit(solution)/shard_map/all_gather | solution.py:121
  23.4 23.2 %copy-start.43 = (f32[128]{0:T(128)}, f32[128]{0:T(128)S(1)}, u32[]{:S(2)}) copy-start(f32[128]{0:T(128)S(1)} %convert_element_type.195) | copy-start | bytes 1540
  28.0 18.7 %copy-start.45 = (f32[128]{0:T(128)}, f32[128]{0:T(128)S(1)}, u32[]{:S(2)}) copy-start(f32[128]{0:T(128)S(1)} %multiply_power_fusion) | copy-start | bytes 1540
  31.9 13.0 %copy-start.50 = (bf16[128]{0:T(256)(128)(2,1)S(1)}, bf16[128]{0:T(256)(128)(2,1)}, u32[]{:S(2)}) copy-start(bf16[128]{0:T(256)(128)(2,1)} %param.27) | copy-start | bytes 772
  31.9 67.1 %all-to-all-start = ((bf16[64,128,256]{2,1,0:T(8,128)(2,1)}), bf16[64,128,256]{2,1,0:T(8,128)(2,1)}, u32[]{:S(2)}, u32[]{:S(2)}) async-start(bf16[64,128,256]{2,1,0:T(8,128)(2,1)} %stack.2), calls=%async_computation | async-start | bytes 8388608 | tf_op jit(solution)/shard_map/all_to_all | solution.py:145
  43.8 155.8 %all-gather.19.cloned.1.call-start = ((), (), s32[]{:S(2)}) async-start(), calls=%async_computation.14 | async-start | bytes 3932160 | tf_op jit(solution)/shard_map/all_gather | solution.py:122
  44.4 589.3 %reduce-scatter.13.cloned.1.call-start = ((), (), s32[]{:S(2)}) async-start(), calls=%async_computation.15 | async-start | bytes 17039360 | tf_op jit(solution)/shard_map/reduce_scatter | solution.py:209
  47.0 62.5 %copy-start.32 = (f32[128,128]{1,0:T(8,128)}, f32[128,128]{1,0:T(8,128)S(1)}, u32[]{:S(2)}) copy-start(f32[128,128]{1,0:T(8,128)S(1)} %get-tuple-element.65) | copy-start | bytes 196612
  47.0 62.5 %copy-start.34 = (f32[128,128]{1,0:T(8,128)}, f32[128,128]{1,0:T(8,128)S(1)}, u32[]{:S(2)}) copy-start(f32[128,128]{1,0:T(8,128)S(1)} %get-tuple-element.66) | copy-start | bytes 196612
  54.1 55.4 %copy-start.37 = (bf16[128,4,128]{2,0,1:T(8,128)(2,1)}, bf16[128,4,128]{2,0,1:T(8,128)(2,1)S(1)}, u32[]{:S(2)}) copy-start(bf16[128,4,128]{2,0,1:T(8,128)(2,1)S(1)} %get-tuple-element.57) | copy-start | bytes 393220
  54.1 55.4 %copy-start.38 = (bf16[128,4,128]{2,0,1:T(8,128)(2,1)}, bf16[128,4,128]{2,0,1:T(8,128)(2,1)S(1)}, u32[]{:S(2)}) copy-start(bf16[128,4,128]{2,0,1:T(8,128)(2,1)S(1)} %get-tuple-element.58) | copy-start | bytes 393220
  150.9 35.2 %copy-start.7 = (bf16[128,640]{1,0:T(8,128)(2,1)}, bf16[128,640]{1,0:T(8,128)(2,1)S(1)}, u32[]{:S(2)}) copy-start(bf16[128,640]{1,0:T(8,128)(2,1)S(1)} %multiply_convert_fusion.5) | copy-start | bytes 491524
  199.6 6.1 copy-start.12
  199.6 6.1 copy-start.29
  210.1 12.6 %copy-start.10 = (f32[128,640]{1,0:T(8,128)}, f32[128,640]{1,0:T(8,128)S(1)}, u32[]{:S(2)}) copy-start(f32[128,640]{1,0:T(8,128)S(1)} %get-tuple-element.50) | copy-start | bytes 983044
  210.3 12.4 %copy-start.20 = (bf16[128,640]{1,0:T(8,128)(2,1)}, bf16[128,640]{1,0:T(8,128)(2,1)S(1)}, u32[]{:S(2)}) copy-start(bf16[128,640]{1,0:T(8,128)(2,1)S(1)} %multiply_convert_fusion.3) | copy-start | bytes 491524
  231.5 4.3 copy-start
  231.5 6.5 copy-start.1
  244.4 8.1 copy-start.33
  244.4 8.1 copy-start.35
  244.4 398.3 %reduce-scatter.15.cloned.1.call-start = ((), (), s32[]{:S(2)}) async-start(), calls=%async_computation.16 | async-start | bytes 1966080 | tf_op jit(solution)/shard_map/reduce_scatter | solution.py:246
  255.4 4.4 copy-start.17
  255.4 403.2 %reduce-scatter.17.cloned.1.call-start = ((), (), s32[]{:S(2)}) async-start(), calls=%async_computation.17 | async-start | bytes 1966080 | tf_op jit(solution)/shard_map/reduce_scatter | solution.py:255
  257.0 418.7 %reduce-scatter.19.cloned.1.call-start = ((), (), s32[]{:S(2)}) async-start(), calls=%async_computation.18 | async-start | bytes 3932160 | tf_op jit(solution)/shard_map/reduce_scatter | solution.py:258
  259.5 433.6 %reduce-scatter.21.cloned.1.call-start = ((), (), s32[]{:S(2)}) async-start(), calls=%async_computation.19 | async-start | bytes 3932160 | tf_op jit(solution)/shard_map/reduce_scatter | solution.py:261
  262.1 372.5 %copy-start.44 = (f32[128]{0:T(128)S(1)}, f32[128]{0:T(128)}, u32[]{:S(2)}) copy-start(f32[128]{0:T(128)} %copy-done.43) | copy-start | bytes 1540
  262.1 372.5 %copy-start.46 = (f32[128]{0:T(128)S(1)}, f32[128]{0:T(128)}, u32[]{:S(2)}) copy-start(f32[128]{0:T(128)} %copy-done.45) | copy-start | bytes 1540
  262.1 372.9 %copy-start.28 = (f32[128,256]{1,0:T(8,128)S(1)}, f32[128,256]{1,0:T(8,128)}, u32[]{:S(2)}) copy-start(f32[128,256]{1,0:T(8,128)} %copy-done.27) | copy-start | bytes 393220
  262.1 372.9 %copy-start.42 = (f32[128]{0:T(128)S(1)}, f32[128]{0:T(128)}, u32[]{:S(2)}) copy-start(f32[128]{0:T(128)} %copy-done.41) | copy-start | bytes 1540
  262.1 374.5 %copy-start.5 = (bf16[640,1024]{1,0:T(8,128)(2,1)S(1)}, bf16[640,1024]{1,0:T(8,128)(2,1)}, u32[]{:S(2)}) copy-start(bf16[640,1024]{1,0:T(8,128)(2,1)} %all-gather.11.cloned.1.call-done) | copy-start | bytes 3932164
  262.2 448.0 %reduce-scatter.23.cloned.1.call-start = ((), (), s32[]{:S(2)}) async-start(), calls=%async_computation.20 | async-start | bytes 3932160 | tf_op jit(solution)/shard_map/reduce_scatter | solution.py:264
  264.6 446.8 %copy-start.23 = (bf16[640,256]{1,0:T(8,128)(2,1)S(1)}, bf16[640,256]{1,0:T(8,128)(2,1)}, u32[]{:S(2)}) copy-start(bf16[640,256]{1,0:T(8,128)(2,1)} %copy-done.22) | copy-start | bytes 983044
  264.6 459.8 %reduce-scatter.25.cloned.1.call-start = ((), (), s32[]{:S(2)}) async-start(), calls=%async_computation.21 | async-start | bytes 491520
  633.6 76.5 %copy-start.36 = (f32[128,512]{1,0:T(8,128)S(1)}, f32[128,512]{1,0:T(8,128)}, u32[]{:S(2)}) copy-start(f32[128,512]{1,0:T(8,128)} %reduce-scatter.13.cloned.1.call-done) | copy-start | bytes 786436
  634.7 79.2 %copy-start.40 = (bf16[640]{0:T(1024)(128)(2,1)S(1)}, bf16[640]{0:T(1024)(128)(2,1)}, u32[]{:S(2)}) copy-start(bf16[640]{0:T(1024)(128)(2,1)} %get-tuple-element.17) | copy-start | bytes 3844
  634.7 79.2 %copy-start.48 = (bf16[256]{0:T(256)(128)(2,1)S(1)}, bf16[256]{0:T(256)(128)(2,1)}, u32[]{:S(2)}) copy-start(bf16[256]{0:T(256)(128)(2,1)} %get-tuple-element.15) | copy-start | bytes 1540
  634.7 82.0 %copy-start.11 = (f32[128,640]{1,0:T(8,128)S(1)}, f32[128,640]{1,0:T(8,128)}, u32[]{:S(2)}) copy-start(f32[128,640]{1,0:T(8,128)} %copy-done.10) | copy-start | bytes 983044
  636.6 102.4 %reduce-scatter.27.cloned.1.call-start = ((), (), s32[]{:S(2)}) async-start(), calls=%async_computation.22 | async-start | bytes 491520
  675.7 64.4 %copy-start.24 = (bf16[640,1024]{1,0:T(8,128)(2,1)S(1)}, bf16[640,1024]{1,0:T(8,128)(2,1)}, u32[]{:S(2)}) copy-start(bf16[640,1024]{1,0:T(8,128)(2,1)} %reduce-scatter.19.cloned.1.call-done) | copy-start | bytes 3932164
  711.7 28.4 %copy-start.25 = (bf16[640,1024]{1,0:T(8,128)(2,1)S(1)}, bf16[640,1024]{1,0:T(8,128)(2,1)}, u32[]{:S(2)}) copy-start(bf16[640,1024]{1,0:T(8,128)(2,1)} %reduce-scatter.21.cloned.1.call-done) | copy-start | bytes 3932164
  (18 other events, 45.4 us)
Sparse Core Ops, SparseCore 0:
  9.7 14.5 all-gather.10
  27.7 109.7 all-gather.8
  139.2 9.5 all-gather.12
  150.3 15.3 all-gather.14
  167.2 15.4 all-gather.16
  184.2 15.3 all-gather.18
  244.5 389.1 reduce-scatter.12
  636.6 6.0 reduce-scatter.14
  645.8 12.8 reduce-scatter.16
  661.4 14.2 reduce-scatter.18
  678.7 14.2 reduce-scatter.20
  695.9 14.2 reduce-scatter.22
  712.6 11.7 reduce-scatter.24
  727.2 11.7 reduce-scatter.26
